TPU v7x, 128 devices: a whole 4x4x4 slice. The times are simulated.
128 devices in a mesh: seq: 64 (over z, y, x), ch: 2 (over core).
Axes of the slice: x: 4, y: 4, z: 4, core: 2. Of those that a mesh axis runs over, the one named last changes fastest.
Arguments:
- tokens: bfloat16 [32768, 2048], P('seq', 'ch'), may hold values from -6 to 6
- in_weight: bfloat16 [2048, 3, 2048], P(None, None, 'ch'), may hold values from -0.125 to 0.125
- short_filter: float32 [3, 3, 2048], P(None, None, 'ch'), may hold values from -3 to 3
- residues: float32 [2048, 16], P('ch'), may hold values from -3 to 3
- rates: float32 [2048, 16], P('ch'), as said below
- out_weight: bfloat16 [2048, 2048], P('ch'), may hold values from -0.1875 to 0.1875
Outputs:
- output: float32 [32768, 2048], P('seq', 'ch')
Inputs may be any that keep to these rules, and one draw needn't show every extreme that they name: `rates`: every rate lies between 0.2 / 32768 and 1 / 30.
All inputs are finite; a program needn't handle non-finite values.
Results may differ from a plain program's by a relative error of at most 0.004.
Values may be sent and summed in bfloat16 or wider, within the bound.
No kernel may reach another device: no remote copies, remote signals or barrier semaphores. Data moves between devices by JAX's collectives and lax.ppermute only.
A program may use at most 192 MiB of HBM per device.

v0:
```python
import jax
import jax.numpy as jnp
from jax import lax
from jax.sharding import PartitionSpec as P


def passed_along(x, axis, by):
    count = lax.axis_size(axis)
    pairs = [(i, i + by) for i in range(count) if 0 <= i + by < count]
    return lax.ppermute(x, axis, pairs)


def carried_in(value, axis, join, neutral):
    count, mine = (lax.axis_size(axis), lax.axis_index(axis))
    pieces = jax.tree.map(lambda part: lax.all_gather(part, axis), value)
    total = jax.tree.map(
        lambda part, zero: jnp.full_like(part, 0) + jnp.asarray(zero, part.dtype), value, neutral
    )

    def turn(position, total):
        longer = join(total, jax.tree.map(lambda part: part[position], pieces))
        return jax.tree.map(lambda new, old: jnp.where(position < mine, new, old), longer, total)

    return lax.fori_loop(0, count - 1, turn, total)


def conv_tables(residues, rates, block_len):
    mode_gain = residues * jnp.sqrt(1.0 - jnp.exp(-2.0 * rates))
    lag_steps = jnp.arange(block_len, dtype=jnp.float32)[:, None, None]
    kernel = jnp.sum(mode_gain * jnp.exp(-rates * lag_steps), axis=-1)
    offsets = jnp.arange(block_len)[:, None] - jnp.arange(block_len)[None, :]
    picked = jnp.take(kernel, jnp.maximum(offsets, 0), axis=0)
    toeplitz = jnp.where((offsets >= 0)[:, :, None], picked, jnp.zeros_like(picked))
    end_weights = jnp.exp(-rates * (block_len - 1.0 - lag_steps))
    lead_weights = mode_gain * jnp.exp(-rates * (lag_steps + 1.0))
    return (toeplitz, end_weights, lead_weights)


def block_terms(source, toeplitz, end_weights, block_len):
    blocks = source.reshape(-1, block_len, source.shape[1])
    local_part = jnp.einsum("tsg,bsg->btg", toeplitz, blocks, precision=lax.Precision.HIGHEST)
    block_ends = jnp.einsum("bsg,sgn->bgn", blocks, end_weights, precision=lax.Precision.HIGHEST)
    return (local_part, block_ends)


def carry_chain(block_ends, step_decay, start_state):

    def advance(carry_state, block_end):
        return (step_decay * carry_state + block_end, carry_state)

    last_state, states = lax.scan(advance, start_state, block_ends)
    return (states, last_state)


def apply_states(lead_weights, states):
    return jnp.einsum("tgn,bgn->btg", lead_weights, states, precision=lax.Precision.HIGHEST)


def combine(earlier, later_pair):
    return (earlier[0] * later_pair[0], later_pair[0] * earlier[1] + later_pair[1])


def on_device(tokens, in_weight, short_filter, residues, rates, out_weight):
    tok_rows = tokens.shape[0]
    channels = in_weight.shape[2]
    model_width = in_weight.shape[0]
    block_len = min(64, tok_rows)
    flat_weight = in_weight.reshape(model_width, 3 * channels)
    projected = jnp.dot(
        lax.all_gather(tokens, "ch", axis=1, tiled=True),
        flat_weight,
        preferred_element_type=jnp.float32,
    )
    projected = projected.reshape(tok_rows, 3, channels)
    before_rows = passed_along(projected[tok_rows - 2 :], "seq", 1)
    padded = jnp.concatenate([before_rows, projected], axis=0)
    filtered = (
        short_filter[0] * padded[2:]
        + short_filter[1] * padded[1:-1]
        + short_filter[2] * padded[:-2]
    )
    queries = filtered[:, 0, :]
    source = filtered[:, 1, :] * filtered[:, 2, :]
    toeplitz, end_weights, lead_weights = conv_tables(residues, rates, block_len)
    local_part, block_ends = block_terms(source, toeplitz, end_weights, block_len)
    step_decay = jnp.exp(-rates * block_len)
    device_decay = jnp.exp(-rates * tok_rows)
    zero_state = jnp.zeros_like(rates)
    states, device_end = carry_chain(block_ends, step_decay, zero_state)
    scanned = carried_in(
        (device_decay, device_end), "seq", combine, (jnp.ones_like(rates), zero_state)
    )
    incoming = scanned[1]
    seeded_states, unused = carry_chain(block_ends, step_decay, incoming)
    convolved = local_part + apply_states(lead_weights, seeded_states)
    convolved = convolved.reshape(tok_rows, channels)
    hidden = (queries * convolved).astype(jnp.bfloat16)
    summed = lax.psum_scatter(
        lax.dot_general(
            out_weight, hidden, (((0,), (1,)), ((), ())), preferred_element_type=jnp.float32
        ),
        "ch",
        scatter_dimension=0,
        tiled=True,
    )
    return summed.T


def solution(mesh):
    return jax.shard_map(
        on_device,
        mesh=mesh,
        in_specs=(
            P("seq", "ch"),
            P(None, None, "ch"),
            P(None, None, "ch"),
            P("ch", None),
            P("ch", None),
            P("ch", None),
        ),
        out_specs=P("seq", "ch"),
        check_vma=False,
    )
```

profile of v0, /device:TPU:1, one launch (start us, length us, event | category | flops | bytes accessed | tf_op | source)
XLA Modules:
  0.0 365.8 jit_solution(14201131429092564687)
XLA Ops:
  7.3 1.5 multiply_exponential_fusion
  8.9 17.2 %copy.31 = bf16[2048,3,1024]{0,2,1:T(8,128)(2,1)} copy(bf16[2048,3,1024]{2,0,1:T(8,128)(2,1)} %param.13) | data formatting | bytes 25165824 | tf_op args[1]
  26.2 10.0 %fusion.38 = f32[512,3072]{1,0:T(8,128)S(1)} fusion(bf16[512,2048]{1,0:T(8,128)(2,1)} %all-gather.6.cloned.1.call-done, bf16[2048,3072]{0,1:T(8,128)(2,1)} %bitcast.73), kind=kOutput, calls=%fused_computation.62 | convolution fusion | flops 6442450944 | bytes 20971520 | tf_op jit(solution)/shard_map/dot_general | solution.py:69
  36.2 2.6 copy-done.1
  38.9 4.2 %collective-permute-start = (f32[2,3,1024]{2,0,1:T(2,128)S(1)}, f32[2,3,1024]{2,0,1:T(2,128)S(1)}, u32[]{:S(2)}, u32[]{:S(2)}) collective-permute-start(f32[2,3,1024]{2,0,1:T(2,128)S(1)} %bitcast.80), channel_id=1, source_target_pairs={{0,2},{2,4},{4,6},{6,8},{8,10},{10,12},{12,14},{14,16},{16,18},{18... | collective-permute-start | bytes 73736 | tf_op jit(solution)/shard_map/ppermute | solution.py:10
  43.4 6.6 %copy.32 = f32[512,3072]{0,1:T(8,128)} copy(f32[512,3072]{1,0:T(8,128)} %copy-done.1) | data formatting | bytes 12582912 | tf_op jit(solution)/shard_map/dot_general | solution.py:69
  50.5 11.5 %fusion.20 = f32[512,3,1024]{0,2,1:T(8,128)S(1)} fusion(f32[2,3,1024]{0,2,1:T(8,128)S(1)} %copy.34, f32[512,3,1024]{0,2,1:T(8,128)} %bitcast.72, f32[3,1024]{1,0:T(4,128)S(1)} %get-tuple-element.256, f32[3,1024]{1,0:T(4,128)S(1)} %get-tuple-element.257, f32[3,1024]{1,0:T(4,128)S(1)} %get-tuple-element.255), kind=kLoop, calls=%fused_computation.32 | loop fusion | flops 11010048 | bytes 12644352 | tf_op jit(solution)/shard_map/add | solution.py:78
  62.0 2.6 copy-done
  64.6 1.8 slice_multiply_fusion
  66.4 1.9 copy.35
  68.4 2.9 copy.40
  71.3 17.2 %fusion.27 = f32[8,1024,16]{2,0,1:T(8,128)} fusion(f32[8,64,1024]{1,0,2:T(8,128)} %copy.40, f32[64]{0:T(128)S(1)} %iota_subtract_fusion.1, f32[1024,16]{1,0:T(8,128)S(1)} %copy.37), kind=kOutput, calls=%fused_computation.42 | convolution fusion | flops 101711872 | bytes 2687232 | tf_op jit(solution)/shard_map/bsg,sgn->bgn/dot_general | solution.py:42
  88.5 2.9 copy.42
  92.8 11.7 %multiply_reduce_fusion = f32[64,1024]{0,1:T(8,128)S(1)} fusion(f32[1024,16]{1,0:T(8,128)S(1)} %copy.37, f32[1024,16]{1,0:T(8,128)S(1)} %copy.36), kind=kLoop, calls=%fused_computation.26 | loop fusion | flops 3080192 | bytes 393216 | tf_op jit(solution)/shard_map/reduce_sum | solution.py:30
  104.9 18.5 %gather_fusion = f32[4096,1024]{1,0:T(8,128)} fusion(f32[64,1024]{1,0:T(8,128)S(1)} %copy.38, s32[4096]{0:T(1024)S(1)} %broadcast_clamp_fusion), kind=kCustom, calls=%fused_computation | custom fusion | bytes 33570816 | tf_op jit(solution)/shard_map/jit(_take)/gather | solution.py:32
  123.4 30.5 %copy.39 = f32[64,64,1024]{1,0,2:T(8,128)} copy(f32[64,64,1024]{2,1,0:T(8,128)} %bitcast.71) | data formatting | bytes 33554432 | tf_op jit(solution)/shard_map/jit(_take)/gather | solution.py:32
  153.9 57.7 %fusion.3 = f32[1024,8,64]{2,1,0:T(8,128)} fusion(f32[8,64,1024]{1,0,2:T(8,128)} %copy.40, f32[64,64,1024]{1,0,2:T(8,128)} %copy.39, pred[64,64]{1,0:T(8,128)(4,1)S(1)} %get-tuple-element.258, pred[64,64]{1,0:T(8,128)(4,1)S(1)} %get-tuple-element.259), kind=kOutput, calls=%fused_computation.12 | convolution fusion | flops 411041792 | bytes 20979712 | tf_op jit(solution)/shard_map/tsg,bsg->btg/dot_general | solution.py:41
  211.7 6.7 %copy.51 = f32[2,8,64,1024]{3,2,1,0:T(8,128)} copy(f32[2,8,64,1024]{3,1,2,0:T(8,128)} %bitcast.78) | data formatting | bytes 8388608
  218.5 6.6 %copy.52 = f32[2,8,64,1024]{3,2,1,0:T(8,128)} copy(f32[2,8,64,1024]{3,1,2,0:T(8,128)} %bitcast.79) | data formatting | bytes 8388608
  225.1 86.8 %while.39 = (s32[]{:T(128)}, f32[1024,16]{0,1:T(8,128)S(1)}, s32[]{:T(128)}, f32[64,1024,16]{1,0,2:T(8,128)}, f32[64,1024,16]{1,0,2:T(8,128)}, /*index=5*/s32[]{:T(128)}, s32[]{:T(128)}) while((s32[]{:T(128)}, f32[1024,16]{0,1:T(8,128)S(1)}, s32[]{:T(128)}, f32[64,1024,16]{1,0,2:T(8,128)}, f32[64,1024,16]{1,0,2:T(8,128)}, ...), condition=%wide.region_4.5_spmd.clone, body=%wide.region_3.4_spmd.clone.sunk | while | flops 65540 | bytes 524397 | solution.py:24
  226.5 1.3 constant_dynamic-slice_fusion.3
  227.9 1.3 constant_dynamic-slice_fusion.3
  229.2 1.3 constant_dynamic-slice_fusion.3
  230.6 1.3 constant_dynamic-slice_fusion.3
  232.0 1.3 constant_dynamic-slice_fusion.3
  233.4 1.3 constant_dynamic-slice_fusion.3
  312.4 2.7 copy.46
  315.1 13.7 %add_bitcast_fusion = f32[8,64,1024]{1,0,2:T(8,128)} fusion(f32[1024,8,64]{2,1,0:T(8,128)} %fusion.3, f32[8,1024,16]{2,0,1:T(8,128)} %copy.46, f32[64]{0:T(128)S(1)} %iota_add_fusion, f32[1024,16]{1,0:T(8,128)S(1)} %copy.37, f32[1024,16]{1,0:T(8,128)S(1)} %copy.36), kind=kOutput, calls=%fused_computation.35 | convolution fusion | flops 103284736 | bytes 4849920 | tf_op jit(solution)/shard_map/tgn,bgn->btg/dot_general | solution.py:56
  328.8 2.8 copy.47
  331.7 1.8 copy.48
  333.5 7.9 %convolution_bitcast_fusion = f32[2048,512]{0,1:T(8,128)} fusion(bf16[1024,2048]{1,0:T(8,128)(2,1)} %param.17, f32[512,1024]{0,1:T(8,128)} %copy.48, f32[512,3,1024]{0,2,1:T(8,128)} %copy-done), kind=kOutput, calls=%fused_computation.41 | convolution fusion | flops 2148532224 | bytes 12582912 | tf_op jit(solution)/shard_map/dot_general | solution.py:99
  341.4 17.6 %reduce-scatter.2.cloned.1.call-done = f32[1024,512]{0,1:T(8,128)} async-done(((f32[2048,512]{0,1:T(8,128)}), f32[1024,512]{0,1:T(8,128)}) %reduce-scatter.2.cloned.1.call-update) | async-done | bytes 2097168 | tf_op jit(solution)/shard_map/reduce_scatter | solution.py:98
  (179 shorter events, 81.3 us)
Async XLA Ops:
  6.5 19.7 %all-gather.6.cloned.1.call-start = ((), (), s32[]{:S(2)}) async-start(), calls=%async_computation.1 | async-start | bytes 3145728 | tf_op jit(solution)/shard_map/all_gather | solution.py:70
  7.3 204.5 %all-gather.8.cloned.1.call-start = ((), (), s32[]{:S(2)}) async-start(), calls=%async_computation.3 | async-start | bytes 4259840 | tf_op jit(solution)/shard_map/all_gather | solution.py:15
  8.9 17.3 %copy-start.3 = (f32[3,3,1024]{2,1,0:T(4,128)S(1)}, f32[3,3,1024]{2,1,0:T(4,128)}, u32[]{:S(2)}) copy-start(f32[3,3,1024]{2,1,0:T(4,128)} %param.14) | copy-start | bytes 110596
  8.9 209.6 %all-gather.10.cloned.1.call-start = ((), (), s32[]{:S(2)}) async-start(), calls=%async_computation.4 | async-start | bytes 4259840 | tf_op jit(solution)/shard_map/all_gather | solution.py:15
  36.2 2.7 copy-start.1
  38.9 11.1 %collective-permute-start = (f32[2,3,1024]{2,0,1:T(2,128)S(1)}, f32[2,3,1024]{2,0,1:T(2,128)S(1)}, u32[]{:S(2)}, u32[]{:S(2)}) collective-permute-start(f32[2,3,1024]{2,0,1:T(2,128)S(1)} %bitcast.80), channel_id=1, source_target_pairs={{0,2},{2,4},{4,6},{6,8},{8,10},{10,12},{12,14},{14,16},{16,18},{18... | collective-permute-start | bytes 73736 | tf_op jit(solution)/shard_map/ppermute | solution.py:10
  62.0 2.6 copy-start
  91.7 0.6 copy-start.2
  92.4 266.7 %reduce-scatter.2.cloned.1.call-start = ((), (), s32[]{:S(2)}) async-start(), calls=%async_computation.2 | async-start | bytes 6291456 | tf_op jit(solution)/shard_map/reduce_scatter | solution.py:98
Sparse Core Ops, SparseCore 0:
  9.0 16.9 all-gather.5
  28.9 68.9 all-gather.7
  100.7 66.3 all-gather.9
  341.6 17.4 reduce-scatter.1
where the time goes:
time: 371 us; the launch traced here: 366 us
  local copies, waits for them, and re-layouts  191 us (51%)
  matrix products  107 us (29%)
  other arithmetic  29.8 us (8%)
  waiting for transfers between devices  18.4 us (5%)
  between operations  13.6 us (4%)
  starting transfers between devices  4.54 us (1%)
    dynamic_slice x63, local copies, waits for them, and re-layouts, turn(): longer = join(total, jax.tree.map(lambda part: part[position], pieces))  82.1 us
    dot_general x1, matrix products, block_terms(): jnp.einsum('tsg,bsg->btg', toeplitz, blocks, precision=lax.Precision.HIGH...  57.7 us
    gather x2, local copies, waits for them, and re-layouts, conv_tables(): picked = jnp.take(kernel, jnp.maximum(offsets, 0), axis=0)  49.1 us
    unnamed x12, local copies, waits for them, and re-layouts  39.4 us
    reduce_scatter x1, waiting for transfers between devices, on_device(): lax.psum_scatter(lax.dot_general(out_weight, hidden, (((0,), (1,)), ((),...  17.6 us
    dot_general x1, matrix products, block_terms(): jnp.einsum('bsg,sgn->bgn', blocks, end_weights, precision=lax.Precision.H...  17.2 us
    dot_general x1, matrix products, apply_states(): jnp.einsum('tgn,bgn->btg', lead_weights, states, precision=lax.Precision....  13.7 us
    reduce_sum x1, other arithmetic, conv_tables(): kernel = jnp.sum(mode_gain * jnp.exp(-rates * lag_steps), axis=-1)  11.7 us
  transfers between devices with their start and end apart: 5, of which 1 were waited for; matrix products, arithmetic and copies ran while one was open for 55% of the time, Pallas kernels for 0%

commit v1 on v0

v1 whole, which is shorter than its diff:
```python
import jax
import jax.numpy as jnp
from jax import lax
from jax.experimental import pallas as pl
from jax.experimental.pallas import tpu as pltpu
from jax.sharding import Mesh, PartitionSpec as P

SEGS = 8
HALO = 16
LANES = 128
SEQ = ("z", "y", "x")
RING = 4
F32 = jnp.float32
BF16 = jnp.bfloat16
VMEM_LIMIT = 48 * 1024 * 1024


def spread(row):
    return jnp.broadcast_to(row, (SEGS, row.shape[-1]))


def filtered_step(taps, now, one, two):
    return taps[0] * now + taps[1] * one + taps[2] * two


def source_kernel(
    ch_ref,
    own_ref,
    other_ref,
    halo_own_ref,
    halo_other_ref,
    w_ref,
    filt_ref,
    rates_ref,
    lhs_ref,
    source_ref,
    ends_ref,
    total_ref,
    proj_ref,
    sems,
):
    rows = own_ref.shape[0]
    half = own_ref.shape[1]
    steps = rows // SEGS
    width = w_ref.shape[2]

    @pl.when(pl.program_id(0) == 0)
    def _():
        mine = pl.multiple_of(ch_ref[0] * half, half)
        theirs = pl.multiple_of((1 - ch_ref[0]) * half, half)
        copies = [
            pltpu.make_async_copy(
                src, lhs_ref.at[pl.ds(row, src.shape[0]), pl.ds(col, half)], sems.at[i]
            )
            for i, (src, row, col) in enumerate(
                (
                    (own_ref, HALO, mine),
                    (other_ref, HALO, theirs),
                    (halo_own_ref, 0, mine),
                    (halo_other_ref, 0, theirs),
                )
            )
        ]
        for copy in copies:
            copy.start()
        for copy in copies:
            copy.wait()

    lhs = lhs_ref[...]
    for j in range(2):
        part = jnp.dot(lhs, w_ref[j], preferred_element_type=F32)
        for i in range(width // LANES):
            proj_ref[j, i] = part[:, i * LANES : (i + 1) * LANES]

    for i in range(width // LANES):
        lanes = pl.ds(i * LANES, LANES)
        taps = [[spread(filt_ref[a, j + 1 : j + 2, lanes]) for a in range(3)] for j in range(2)]
        decays = [spread(jnp.exp(-rates_ref[n : n + 1, lanes])) for n in range(rates_ref.shape[0])]

        def at(j, t):
            return proj_ref[j, i, pl.ds(HALO + t, SEGS, stride=steps), :]

        def body(t, carry):
            k1, k2, v1, v2, states = carry
            k0, v0 = at(0, t), at(1, t)
            src = filtered_step(taps[0], k0, k1, k2) * filtered_step(taps[1], v0, v1, v2)
            source_ref[pl.ds(pl.multiple_of(t * SEGS, SEGS), SEGS), lanes] = src
            states = tuple(d * s + src for d, s in zip(decays, states))
            return k0, k1, v0, v1, states

        zero = jnp.zeros((SEGS, LANES), F32)
        carry = (at(0, -1), at(0, -2), at(1, -1), at(1, -2), (zero,) * len(decays))
        states = lax.fori_loop(0, steps, body, carry, unroll=8)[4]
        later = (SEGS - 1 - lax.broadcasted_iota(jnp.int32, (SEGS, LANES), 0)).astype(F32) * steps
        for n, state in enumerate(states):
            ends_ref[n * SEGS : (n + 1) * SEGS, lanes] = state
            weight = jnp.exp(-spread(rates_ref[n : n + 1, lanes]) * later)
            total_ref[n : n + 1, lanes] = jnp.sum(state * weight, axis=0, keepdims=True)


def source_call(ch, own, other, halo_own, halo_other, weight, filt, rates, width=256):
    rows, half = own.shape
    channels = weight.shape[2]
    modes = rates.shape[0]
    full = 2 * half
    grid_spec = pltpu.PrefetchScalarGridSpec(
        num_scalar_prefetch=1,
        grid=(channels // width,),
        in_specs=[pl.BlockSpec(memory_space=pl.ANY)] * 4
        + [
            pl.BlockSpec((pl.Element(2), pl.Element(full), pl.Element(width)), lambda i, c: (1, 0, i * width)),
            pl.BlockSpec((3, 3, width), lambda i, c: (0, 0, i)),
            pl.BlockSpec((modes, width), lambda i, c: (0, i)),
        ],
        out_specs=[
            pl.BlockSpec((HALO + rows, full), lambda i, c: (0, 0)),
            pl.BlockSpec((rows, width), lambda i, c: (0, i)),
            pl.BlockSpec((modes * SEGS, width), lambda i, c: (0, i)),
            pl.BlockSpec((modes, width), lambda i, c: (0, i)),
        ],
        scratch_shapes=[
            pltpu.VMEM((2, width // LANES, HALO + rows, LANES), F32),
            pltpu.SemaphoreType.DMA((4,)),
        ],
    )
    return pl.pallas_call(
        source_kernel,
        grid_spec=grid_spec,
        out_shape=[
            jax.ShapeDtypeStruct((HALO + rows, full), BF16),
            jax.ShapeDtypeStruct((rows, channels), F32),
            jax.ShapeDtypeStruct((modes * SEGS, channels), F32),
            jax.ShapeDtypeStruct((modes, channels), F32),
        ],
        compiler_params=pltpu.CompilerParams(vmem_limit_bytes=VMEM_LIMIT),
        name="source",
    )(ch, own, other, halo_own, halo_other, weight, filt, rates)


def query_kernel(lhs_ref, w_ref, filt_ref, query_ref, proj_ref):
    steps = query_ref.shape[0] // SEGS
    width = w_ref.shape[2]
    part = jnp.dot(lhs_ref[...], w_ref[0], preferred_element_type=F32)
    for i in range(width // LANES):
        proj_ref[i] = part[:, i * LANES : (i + 1) * LANES]
    for i in range(width // LANES):
        lanes = pl.ds(i * LANES, LANES)
        taps = [spread(filt_ref[a, 0:1, lanes]) for a in range(3)]

        def at(t):
            return proj_ref[i, pl.ds(HALO + t, SEGS, stride=steps), :]

        def body(t, carry):
            q1, q2 = carry
            q0 = at(t)
            query_ref[pl.ds(pl.multiple_of(t * SEGS, SEGS), SEGS), lanes] = filtered_step(
                taps, q0, q1, q2
            )
            return q0, q1

        lax.fori_loop(0, steps, body, (at(-1), at(-2)), unroll=8)


def query_call(lhs, weight, filt, width=256):
    rows = lhs.shape[0] - HALO
    full, channels = weight.shape[1:]
    return pl.pallas_call(
        query_kernel,
        grid=(channels // width,),
        in_specs=[
            pl.BlockSpec(lhs.shape, lambda i: (0, 0)),
            pl.BlockSpec((1, full, width), lambda i: (0, 0, i)),
            pl.BlockSpec((3, 3, width), lambda i: (0, 0, i)),
        ],
        out_specs=pl.BlockSpec((rows, width), lambda i: (0, i)),
        out_shape=jax.ShapeDtypeStruct((rows, channels), F32),
        scratch_shapes=[pltpu.VMEM((width // LANES, HALO + rows, LANES), F32)],
        compiler_params=pltpu.CompilerParams(vmem_limit_bytes=VMEM_LIMIT),
        name="query",
    )(lhs, weight, filt)


def local_kernel(source_ref, rates_ref, gain_ref, local_ref):
    steps = source_ref.shape[0] // SEGS
    modes = rates_ref.shape[0]
    decays = [spread(jnp.exp(-rates_ref[n : n + 1])) for n in range(modes)]
    gains = [spread(gain_ref[n : n + 1]) for n in range(modes)]

    def body(t, states):
        rows = pl.ds(pl.multiple_of(t * SEGS, SEGS), SEGS)
        src = source_ref[rows]
        states = tuple(d * s + src for d, s in zip(decays, states))
        parts = [g * s for g, s in zip(gains, states)]
        while len(parts) > 1:
            parts = [a + b for a, b in zip(parts[::2], parts[1::2])]
        local_ref[rows] = parts[0]
        return states

    zero = jnp.zeros((SEGS, LANES), F32)
    lax.fori_loop(0, steps, body, (zero,) * modes, unroll=8)


def local_call(source, rates, gain):
    rows, channels = source.shape
    modes = rates.shape[0]
    return pl.pallas_call(
        local_kernel,
        grid=(channels // LANES,),
        in_specs=[
            pl.BlockSpec((rows, LANES), lambda i: (0, i)),
            pl.BlockSpec((modes, LANES), lambda i: (0, i)),
            pl.BlockSpec((modes, LANES), lambda i: (0, i)),
        ],
        out_specs=pl.BlockSpec((rows, LANES), lambda i: (0, i)),
        out_shape=jax.ShapeDtypeStruct((rows, channels), F32),
        compiler_params=pltpu.CompilerParams(vmem_limit_bytes=VMEM_LIMIT),
        name="local",
    )(source, rates, gain)


def hidden_kernel(ends_ref, into_ref, local_ref, query_ref, rates_ref, gain_ref, hidden_ref):
    steps = local_ref.shape[0] // SEGS
    modes = rates_ref.shape[0]
    seg = lax.broadcasted_iota(jnp.int32, (SEGS, LANES), 0)
    decays, leads = [], []
    for n in range(modes):
        rate = spread(rates_ref[n : n + 1])
        state = pltpu.roll(ends_ref[n * SEGS : (n + 1) * SEGS], 1, 0)
        state = jnp.where(seg == 0, spread(into_ref[n : n + 1]), state)
        for hop in (1, 2, 4):
            earlier = pltpu.roll(state, hop, 0) * jnp.exp(-rate * float(steps * hop))
            state = state + jnp.where(seg >= hop, earlier, 0.0)
        decays.append(jnp.exp(-rate))
        leads.append(spread(gain_ref[n : n + 1]) * state)

    def body(t, leads):
        halves = []
        for u in range(2):
            rows = pl.ds(pl.multiple_of((2 * t + u) * SEGS, SEGS), SEGS)
            leads = tuple(d * s for d, s in zip(decays, leads))
            parts = list(leads)
            while len(parts) > 1:
                parts = [a + b for a, b in zip(parts[::2], parts[1::2])]
            halves.append(query_ref[rows] * (local_ref[rows] + parts[0]))
        rows = pl.ds(pl.multiple_of(2 * t * SEGS, 2 * SEGS), 2 * SEGS)
        hidden_ref[rows] = jnp.concatenate(halves, axis=0).astype(BF16)
        return leads

    lax.fori_loop(0, steps // 2, body, tuple(leads), unroll=4)


def hidden_call(ends, into, local, query, rates, gain):
    rows, channels = local.shape
    modes = rates.shape[0]

    def spec(count):
        return pl.BlockSpec((count, LANES), lambda i: (0, i))

    return pl.pallas_call(
        hidden_kernel,
        grid=(channels // LANES,),
        in_specs=[spec(modes * SEGS), spec(modes), spec(rows), spec(rows), spec(modes), spec(modes)],
        out_specs=spec(rows),
        out_shape=jax.ShapeDtypeStruct((rows, channels), BF16),
        compiler_params=pltpu.CompilerParams(vmem_limit_bytes=VMEM_LIMIT),
        name="hidden",
    )(ends, into, local, query, rates, gain)


def output_kernel(ch_ref, own_ref, other_ref, w_own_ref, w_other_ref, out_ref, acc_ref):
    rows, width = out_ref.shape
    steps = rows // SEGS
    part = jnp.dot(own_ref[...], w_own_ref[...], preferred_element_type=F32)
    part = part + jnp.dot(other_ref[...], w_other_ref[...], preferred_element_type=F32)
    for i in range(width // LANES):
        acc_ref[i] = part[:, i * LANES : (i + 1) * LANES]
    for i in range(width // LANES):
        for j in range(SEGS):
            out_ref[j * steps : (j + 1) * steps, i * LANES : (i + 1) * LANES] = acc_ref[
                i, pl.ds(j, steps, stride=SEGS), :
            ]


def output_call(ch, own, other, w_own, w_other, width=256):
    rows, channels = own.shape
    columns = w_own.shape[1] // 2
    tiles = columns // width
    grid_spec = pltpu.PrefetchScalarGridSpec(
        num_scalar_prefetch=1,
        grid=(tiles,),
        in_specs=[
            pl.BlockSpec((rows, channels), lambda i, c: (0, 0)),
            pl.BlockSpec((rows, channels), lambda i, c: (0, 0)),
            pl.BlockSpec((channels, width), lambda i, c: (0, c[0] * tiles + i)),
            pl.BlockSpec((channels, width), lambda i, c: (0, c[0] * tiles + i)),
        ],
        out_specs=pl.BlockSpec((rows, width), lambda i, c: (0, i)),
        scratch_shapes=[pltpu.VMEM((width // LANES, rows, LANES), F32)],
    )
    return pl.pallas_call(
        output_kernel,
        grid_spec=grid_spec,
        out_shape=jax.ShapeDtypeStruct((rows, columns), F32),
        compiler_params=pltpu.CompilerParams(vmem_limit_bytes=VMEM_LIMIT),
        name="output",
    )(ch, own, other, w_own, w_other)


def swapped(x):
    return lax.ppermute(x, "ch", [(0, 1), (1, 0)])


def from_before(x, crossed):
    count = RING**3
    pairs = [
        (2 * i + c, 2 * (i + 1) + (1 - c if crossed else c))
        for i in range(count - 1)
        for c in range(2)
    ]
    return lax.ppermute(x, (*SEQ, "ch"), pairs)


def ring_level(state, axis, rates, tokens):
    here = lax.axis_index(axis)
    sent = state.astype(BF16)
    arrived = [
        lax.ppermute(sent, axis, [(i, (i + k) % RING) for i in range(RING)]).astype(F32)
        for k in range(1, RING)
    ]
    before = jnp.zeros_like(state)
    total = state * jnp.exp(-rates * (tokens * (RING - 1 - here)).astype(F32))
    for k, part in zip(range(1, RING), arrived):
        weight = jnp.where(k <= here, jnp.exp(-rates * float(tokens * (k - 1))), 0.0)
        before = before + weight * part
        place = (here - k) % RING
        total = total + part * jnp.exp(-rates * (tokens * (RING - 1 - place)).astype(F32))
    return before, total


def on_device(tokens, in_weight, short_filter, residues, rates, out_weight):
    rows = tokens.shape[0]
    ch = lax.axis_index("ch").astype(jnp.int32).reshape(1)
    weight = in_weight.transpose(1, 0, 2)
    rates = rates.T
    gain = residues.T * jnp.sqrt(1.0 - jnp.exp(-2.0 * rates))

    other = swapped(tokens)
    last = tokens[rows - HALO :]
    halo_own = from_before(last, False)
    halo_other = from_before(last, True)
    out_weight_other = swapped(out_weight)

    lhs, source, ends, total = source_call(
        ch, tokens, other, halo_own, halo_other, weight, short_filter, rates
    )
    query = query_call(lhs, weight, short_filter)
    local = local_call(source, rates, gain)

    into = jnp.zeros_like(total)
    after = 0
    span = rows
    for axis in reversed(SEQ):
        before, total = ring_level(total, axis, rates, span)
        into = into + before * jnp.exp(-rates * jnp.asarray(after, F32))
        after = after + span * lax.axis_index(axis)
        span = span * RING

    hidden = hidden_call(ends, into, local, query, rates, gain)
    return output_call(ch, hidden, swapped(hidden), out_weight, out_weight_other)


def solution(mesh):
    cube = Mesh(mesh.devices.reshape(RING, RING, RING, 2), (*SEQ, "ch"))
    return jax.shard_map(
        on_device,
        mesh=cube,
        in_specs=(
            P(SEQ, "ch"),
            P(None, None, "ch"),
            P(None, None, "ch"),
            P("ch", None),
            P("ch", None),
            P("ch", None),
        ),
        out_specs=P(SEQ, "ch"),
        check_vma=False,
    )
```

time: 371 us -> 78.5 us (0.21); the launches traced: 366 us -> 78 us
  local copies, waits for them, and re-layouts: 191 us -> 6.04 us
  matrix products: 107 us -> 0 us
  Pallas kernels: 0 us -> 35.4 us
  other arithmetic: 29.8 us -> 0.36 us
  starting transfers between devices: 4.54 us -> 25.4 us
  between operations: 13.6 us -> 0.14 us
  waiting for transfers between devices: 18.4 us -> 10.7 us
    dot_general x5 -> x0, matrix products: 107 us -> none  [the longest x1 57.7 us: block_terms(): jnp.einsum('tsg,bsg->btg', toeplitz, blocks, precision=lax.Precision.HIGH...]
    dynamic_slice x63 -> x0, local copies, waits for them, and re-layouts: 82.1 us -> none  [turn(): longer = join(total, jax.tree.map(lambda part: part[position], pieces))]
    gather x2 -> x0, local copies, waits for them, and re-layouts: 49.1 us -> none  [conv_tables(): picked = jnp.take(kernel, jnp.maximum(offsets, 0), axis=0)]
    pallas_call x0 -> x5, Pallas kernels: none -> 35.4 us  [the longest x1 13.8 us: source_call(): pl.pallas_call(source_kernel, grid_spec=grid_spec, out_shape=[jax.ShapeDt...]
    unnamed x12 -> x18, local copies, waits for them, and re-layouts: 39.4 us -> 5.28 us
    ppermute x1 -> x14, starting transfers between devices: 4.24 us -> 25.4 us  [the longest x9 12.4 us: ring_level(): lax.ppermute(sent, axis, [(i, (i + k) % RING) for i in range(RING)])]
    reduce_scatter x1 -> x0, waiting for transfers between devices: 17.6 us -> none  [on_device(): lax.psum_scatter(lax.dot_general(out_weight, hidden, (((0,), (1,)), ((),...]
    reduce_sum x1 -> x0, other arithmetic: 11.7 us -> none  [conv_tables(): kernel = jnp.sum(mode_gain * jnp.exp(-rates * lag_steps), axis=-1)]
  transfers between devices with their start and end apart: 5 -> 14, of which waited for: 1 -> 7; matrix products, arithmetic and copies ran while one was open for 55% -> 1% of each run, Pallas kernels for 0% -> 38%
where the time goes in v1:
time: 78.5 us; the launch traced here: 78 us
  Pallas kernels  35.4 us (45%)
  starting transfers between devices  25.4 us (32%)
  waiting for transfers between devices  10.7 us (14%)
  local copies, waits for them, and re-layouts  6.04 us (8%)
    pallas_call x1, Pallas kernels, source_call(): pl.pallas_call(source_kernel, grid_spec=grid_spec, out_shape=[jax.ShapeDt...  13.8 us
    ppermute x9, starting transfers between devices, ring_level(): lax.ppermute(sent, axis, [(i, (i + k) % RING) for i in range(RING)])  12.4 us
    ppermute x9, waiting for transfers between devices, ring_level(): lax.ppermute(sent, axis, [(i, (i + k) % RING) for i in range(RING)])  7.37 us
    ppermute x2, starting transfers between devices, from_before(): return lax.ppermute(x, (*SEQ, 'ch'), pairs)  6.7 us
    ppermute x3, starting transfers between devices, swapped(): return lax.ppermute(x, 'ch', [(0, 1), (1, 0)])  6.35 us
    pallas_call x1, Pallas kernels, query_call(): pl.pallas_call(query_kernel, grid=(channels // width,), in_specs=[pl.Bloc...  6.19 us
    pallas_call x1, Pallas kernels, output_call(): pl.pallas_call(output_kernel, grid_spec=grid_spec, out_shape=jax.ShapeDty...  5.78 us
    pallas_call x1, Pallas kernels, local_call(): pl.pallas_call(local_kernel, grid=(channels // LANES,), in_specs=[pl.Bloc...  5.31 us
  transfers between devices with their start and end apart: 14, of which 7 were waited for; matrix products, arithmetic and copies ran while one was open for 1% of the time, Pallas kernels for 38%

profile of v1, /device:TPU:1, one launch (start us, length us, event | category | flops | bytes accessed | tf_op | source)
XLA Modules:
  0.0 78.0 jit_solution(7227278282355249946)
XLA Ops:
  0.0 1.4 %collective-permute-start.13 = (bf16[1024,2048]{1,0:T(8,128)(2,1)}, bf16[1024,2048]{1,0:T(8,128)(2,1)}, u32[]{:S(2)}, u32[]{:S(2)}) collective-permute-start(bf16[1024,2048]{1,0:T(8,128)(2,1)} %w_own_ref.1), channel_id=1, source_target_pairs={{0,1},{1,0},{2,3},{3,2},{4,5},{5,4},{6,7},{7,6},{8,9},{9,8},{10,11... | collective-permute-start | bytes 12582920 | tf_op jit(solution)/shard_map/ppermute | solution.py:310
  1.4 0.8 slice.3
  2.2 3.6 %collective-permute-start.2 = (bf16[16,1024]{1,0:T(8,128)(2,1)S(1)}, bf16[16,1024]{1,0:T(8,128)(2,1)S(1)}, u32[]{:S(2)}, u32[]{:S(2)}) collective-permute-start(bf16[16,1024]{1,0:T(8,128)(2,1)S(1)} %slice.3), channel_id=1, source_target_pairs={{0,3},{1,2},{2,5},{3,4},{4,7},{5,6},{6,9},{7,8},{8,11},{9,10},{10,... | collective-permute-start | bytes 98312 | tf_op jit(solution)/shard_map/ppermute | solution.py:320
  5.8 3.1 %collective-permute-start.1 = (bf16[16,1024]{1,0:T(8,128)(2,1)S(1)}, bf16[16,1024]{1,0:T(8,128)(2,1)S(1)}, u32[]{:S(2)}, u32[]{:S(2)}) collective-permute-start(bf16[16,1024]{1,0:T(8,128)(2,1)S(1)} %slice.3), channel_id=1, source_target_pairs={{0,2},{1,3},{2,4},{3,5},{4,6},{5,7},{6,8},{7,9},{8,10},{9,11},{10,... | collective-permute-start | bytes 98312 | tf_op jit(solution)/shard_map/ppermute | solution.py:320
  8.9 1.0 %collective-permute-done.1.halo_own_ref = bf16[16,1024]{1,0:T(8,128)(2,1)S(1)} collective-permute-done((bf16[16,1024]{1,0:T(8,128)(2,1)S(1)}, bf16[16,1024]{1,0:T(8,128)(2,1)S(1)}, u32[]{:S(2)}, u32[]{:S(2)}) %collective-permute-start.1) | collective-permute-done | bytes 32800 | tf_op jit(solution)/shard_map/ppermute | solution.py:320
  9.9 0.8 %copy-done = f32[1024,16]{0,1:T(8,128)S(1)} copy-done((f32[1024,16]{0,1:T(8,128)S(1)}, f32[1024,16]{0,1:T(8,128)}, u32[]{:S(2)}) %copy-start) | copy-done | bytes 65560
  10.8 1.2 %copy-done.3 = bf16[512,1024]{1,0:T(8,128)(2,1)S(1)} copy-done((bf16[512,1024]{1,0:T(8,128)(2,1)S(1)}, bf16[512,1024]{1,0:T(8,128)(2,1)}, u32[]{:S(2)}) %copy-start.3) | copy-done | bytes 1048600
  12.0 0.8 %copy-done.6 = f32[3,3,1024]{2,1,0:T(4,128)S(1)} copy-done((f32[3,3,1024]{2,1,0:T(4,128)S(1)}, f32[3,3,1024]{2,1,0:T(4,128)}, u32[]{:S(2)}) %copy-start.6) | copy-done | bytes 36888
  12.8 13.8 %source.1 = (bf16[528,2048]{1,0:T(8,128)(2,1)}, f32[512,1024]{1,0:T(8,128)S(1)}, f32[128,1024]{1,0:T(8,128)S(1)}, f32[16,1024]{1,0:T(8,128)S(1)}) custom-call(s32[1]{0:T(128)} %bitcast.ch_ref, bf16[512,1024]{1,0:T(8,128)(2,1)S(1)} %copy-done.3, bf16[512,1024]{1,0:T(8,128)(2,1)S(1)} %collective-permute-done.other_ref, ...), custom_call_target="tpu_custom_call" | custom-call | tf_op jit(solution)/shard_map/source/pallas_call | solution.py:126
  26.6 0.8 %copy-done.4 = f32[128,1024]{1,0:T(8,128)} copy-done((f32[128,1024]{1,0:T(8,128)}, f32[128,1024]{1,0:T(8,128)S(1)}, u32[]{:S(2)}) %copy-start.4) | copy-done | bytes 524312
  27.4 3.0 %collective-permute-start.5 = (bf16[16,1024]{1,0:T(8,128)(2,1)S(1)}, bf16[16,1024]{1,0:T(8,128)(2,1)S(1)}, u32[]{:S(2)}, u32[]{:S(2)}) collective-permute-start(bf16[16,1024]{1,0:T(8,128)(2,1)S(1)} %convert_element_type.66), channel_id=1, source_target_pairs={{0,6},{2,0},{4,2},{6,4},{1,7},{3,1},{5,3},{7,5},{8,14},{10,8},{12,... | collective-permute-start | bytes 98312 | tf_op jit(solution)/shard_map/ppermute | solution.py:327
  30.4 0.5 collective-permute-start.4
  30.9 0.3 collective-permute-start.3
  31.2 0.2 collective-permute-done.5
  31.4 3.3 %collective-permute-done.4 = bf16[16,1024]{1,0:T(8,128)(2,1)S(1)} collective-permute-done((bf16[16,1024]{1,0:T(8,128)(2,1)S(1)}, bf16[16,1024]{1,0:T(8,128)(2,1)S(1)}, u32[]{:S(2)}, u32[]{:S(2)}) %collective-permute-start.4) | collective-permute-done | bytes 32800 | tf_op jit(solution)/shard_map/ppermute | solution.py:327
  34.7 0.3 collective-permute-done.3
  35.1 3.0 %collective-permute-start.8 = (bf16[16,1024]{1,0:T(8,128)(2,1)S(1)}, bf16[16,1024]{1,0:T(8,128)(2,1)S(1)}, u32[]{:S(2)}, u32[]{:S(2)}) collective-permute-start(bf16[16,1024]{1,0:T(8,128)(2,1)S(1)} %get-tuple-element.14), channel_id=1, source_target_pairs={{0,24},{8,0},{16,8},{24,16},{1,25},{9,1},{17,9},{25,17},{2,26},{10... | collective-permute-start | bytes 98312 | tf_op jit(solution)/shard_map/ppermute | solution.py:327
  38.1 0.3 collective-permute-start.7
  38.4 0.7 collective-permute-start.6
  39.1 3.3 %collective-permute-done.7 = bf16[16,1024]{1,0:T(8,128)(2,1)S(1)} collective-permute-done((bf16[16,1024]{1,0:T(8,128)(2,1)S(1)}, bf16[16,1024]{1,0:T(8,128)(2,1)S(1)}, u32[]{:S(2)}, u32[]{:S(2)}) %collective-permute-start.7) | collective-permute-done | bytes 32800 | tf_op jit(solution)/shard_map/ppermute | solution.py:327
  42.4 0.3 collective-permute-done.6
  42.7 0.1 fusion.14
  42.8 3.8 %collective-permute-start.11 = (bf16[16,1024]{1,0:T(8,128)(2,1)S(1)}, bf16[16,1024]{1,0:T(8,128)(2,1)S(1)}, u32[]{:S(2)}, u32[]{:S(2)}) collective-permute-start(bf16[16,1024]{1,0:T(8,128)(2,1)S(1)} %fusion.14), channel_id=1, source_target_pairs={{0,96},{32,0},{64,32},{96,64},{1,97},{33,1},{65,33},{97,65},{2,98}... | collective-permute-start | bytes 98312 | tf_op jit(solution)/shard_map/ppermute | solution.py:327
  46.6 0.7 collective-permute-start.9
  47.4 1.6 %copy-done.2 = bf16[528,2048]{1,0:T(8,128)(2,1)S(1)} copy-done((bf16[528,2048]{1,0:T(8,128)(2,1)S(1)}, bf16[528,2048]{1,0:T(8,128)(2,1)}, u32[]{:S(2)}) %copy-start.2) | copy-done | bytes 2162712
  49.0 6.2 %query.1.query_ref = f32[512,1024]{1,0:T(8,128)S(1)} custom-call(bf16[528,2048]{1,0:T(8,128)(2,1)S(1)} %copy-done.2, bf16[3,2048,1024]{2,1,0:T(8,128)(2,1)} %bitcast.17, f32[3,3,1024]{2,1,0:T(4,128)S(1)} %copy-done.7), custom_call_target="tpu_custom_call" | custom-call | tf_op jit(solution)/shard_map/query/pallas_call | solution.py:167
  55.2 5.3 %local.1.local_ref = f32[512,1024]{1,0:T(8,128)S(1)} custom-call(f32[512,1024]{1,0:T(8,128)S(1)} %get-tuple-element.11.source_ref, f32[16,1024]{1,0:T(8,128)S(1)} %bitcast.14, f32[16,1024]{1,0:T(8,128)S(1)} %get-tuple-element.13.gain_ref), custom_call_target="tpu_custom_call" | custom-call | tf_op jit(solution)/shard_map/local/pallas_call | solution.py:206
  60.5 0.2 fusion.4.into_ref
  60.7 4.3 %hidden.1.own_ref = bf16[512,1024]{1,0:T(8,128)(2,1)S(1)} custom-call(f32[128,1024]{1,0:T(8,128)S(1)} %copy-done.5, f32[16,1024]{1,0:T(8,128)S(1)} %fusion.4.into_ref, f32[512,1024]{1,0:T(8,128)S(1)} %local.1.local_ref, f32[512,1024]{1,0:T(8,128)S(1)} %query.1.query_ref, f32[16,1024]{1,0:T(8,128)S(1)} %bitcast.15, f32[16,1024]{1,0:T(8,128)S(1)} %get-tuple-element.13.gain_ref), custom_call_target="tpu_custom_call" | custom-call | tf_op jit(solution)/shard_map/hidden/pallas_call | solution.py:259
  65.0 4.9 %collective-permute-start.12 = (bf16[512,1024]{1,0:T(8,128)(2,1)S(1)}, bf16[512,1024]{1,0:T(8,128)(2,1)S(1)}, u32[]{:S(2)}, u32[]{:S(2)}) collective-permute-start(bf16[512,1024]{1,0:T(8,128)(2,1)S(1)} %hidden.1.own_ref), channel_id=1, source_target_pairs={{0,1},{1,0},{2,3},{3,2},{4,5},{5,4},{6,7},{7,6},{8,9},{9,8},{10,11... | collective-permute-start | bytes 3145736 | tf_op jit(solution)/shard_map/ppermute | solution.py:310
  69.9 2.3 %collective-permute-done.12.other_ref = bf16[512,1024]{1,0:T(8,128)(2,1)S(1)} collective-permute-done((bf16[512,1024]{1,0:T(8,128)(2,1)S(1)}, bf16[512,1024]{1,0:T(8,128)(2,1)S(1)}, u32[]{:S(2)}, u32[]{:S(2)}) %collective-permute-start.12) | collective-permute-done | bytes 1048608 | tf_op jit(solution)/shard_map/ppermute | solution.py:310
  72.2 5.8 %output.1 = f32[512,1024]{1,0:T(8,128)} custom-call(s32[1]{0:T(128)} %bitcast.ch_ref, bf16[512,1024]{1,0:T(8,128)(2,1)S(1)} %hidden.1.own_ref, bf16[512,1024]{1,0:T(8,128)(2,1)S(1)} %collective-permute-done.12.other_ref, bf16[1024,2048]{1,0:T(8,128)(2,1)} %w_own_ref.1, bf16[1024,2048]{1,0:T(8,128)(2,1)} %collective-permute-done.13.w_other_ref), custom_call_target="tpu_custom_call" | custom-call | tf_op jit(solution)/shard_map/output/pallas_call | solution.py:300
  (24 shorter events, 0.1 us)
Async XLA Ops:
  0.0 72.2 %collective-permute-start.13 = (bf16[1024,2048]{1,0:T(8,128)(2,1)}, bf16[1024,2048]{1,0:T(8,128)(2,1)}, u32[]{:S(2)}, u32[]{:S(2)}) collective-permute-start(bf16[1024,2048]{1,0:T(8,128)(2,1)} %w_own_ref.1), channel_id=1, source_target_pairs={{0,1},{1,0},{2,3},{3,2},{4,5},{5,4},{6,7},{7,6},{8,9},{9,8},{10,11... | collective-permute-start | bytes 12582920 | tf_op jit(solution)/shard_map/ppermute | solution.py:310
  1.4 8.5 %collective-permute-start = (bf16[512,1024]{1,0:T(8,128)(2,1)}, bf16[512,1024]{1,0:T(8,128)(2,1)S(1)}, u32[]{:S(2)}, u32[]{:S(2)}) collective-permute-start(bf16[512,1024]{1,0:T(8,128)(2,1)} %own_ref.1), channel_id=1, source_target_pairs={{0,1},{1,0},{2,3},{3,2},{4,5},{5,4},{6,7},{7,6},{8,9},{9,8},{10,11... | collective-permute-start | bytes 3145736 | tf_op jit(solution)/shard_map/ppermute | solution.py:310
  2.2 6.7 %collective-permute-start.2 = (bf16[16,1024]{1,0:T(8,128)(2,1)S(1)}, bf16[16,1024]{1,0:T(8,128)(2,1)S(1)}, u32[]{:S(2)}, u32[]{:S(2)}) collective-permute-start(bf16[16,1024]{1,0:T(8,128)(2,1)S(1)} %slice.3), channel_id=1, source_target_pairs={{0,3},{1,2},{2,5},{3,4},{4,7},{5,6},{6,9},{7,8},{8,11},{9,10},{10,... | collective-permute-start | bytes 98312 | tf_op jit(solution)/shard_map/ppermute | solution.py:320
  5.8 4.1 %collective-permute-start.1 = (bf16[16,1024]{1,0:T(8,128)(2,1)S(1)}, bf16[16,1024]{1,0:T(8,128)(2,1)S(1)}, u32[]{:S(2)}, u32[]{:S(2)}) collective-permute-start(bf16[16,1024]{1,0:T(8,128)(2,1)S(1)} %slice.3), channel_id=1, source_target_pairs={{0,2},{1,3},{2,4},{3,5},{4,6},{5,7},{6,8},{7,9},{8,10},{9,11},{10,... | collective-permute-start | bytes 98312 | tf_op jit(solution)/shard_map/ppermute | solution.py:320
  9.9 0.8 %copy-start = (f32[1024,16]{0,1:T(8,128)S(1)}, f32[1024,16]{0,1:T(8,128)}, u32[]{:S(2)}) copy-start(f32[1024,16]{0,1:T(8,128)} %param.10) | copy-start | bytes 196612
  10.8 1.2 %copy-start.3 = (bf16[512,1024]{1,0:T(8,128)(2,1)S(1)}, bf16[512,1024]{1,0:T(8,128)(2,1)}, u32[]{:S(2)}) copy-start(bf16[512,1024]{1,0:T(8,128)(2,1)} %own_ref.1) | copy-start | bytes 3145732
  12.0 0.8 %copy-start.6 = (f32[3,3,1024]{2,1,0:T(4,128)S(1)}, f32[3,3,1024]{2,1,0:T(4,128)}, u32[]{:S(2)}) copy-start(f32[3,3,1024]{2,1,0:T(4,128)} %filt_ref.3) | copy-start | bytes 110596
  12.8 22.2 %copy-start.1 = (f32[1024,16]{0,1:T(8,128)S(1)}, f32[1024,16]{0,1:T(8,128)}, u32[]{:S(2)}) copy-start(f32[1024,16]{0,1:T(8,128)} %param.10) | copy-start | bytes 196612
  12.8 22.2 %copy-start.8 = (f32[1024,16]{0,1:T(8,128)S(1)}, f32[1024,16]{0,1:T(8,128)}, u32[]{:S(2)}) copy-start(f32[1024,16]{0,1:T(8,128)} %param.9) | copy-start | bytes 196612
  12.8 34.6 %copy-start.7 = (f32[3,3,1024]{2,1,0:T(4,128)S(1)}, f32[3,3,1024]{2,1,0:T(4,128)}, u32[]{:S(2)}) copy-start(f32[3,3,1024]{2,1,0:T(4,128)} %filt_ref.3) | copy-start | bytes 110596
  26.6 0.8 %copy-start.4 = (f32[128,1024]{1,0:T(8,128)}, f32[128,1024]{1,0:T(8,128)S(1)}, u32[]{:S(2)}) copy-start(f32[128,1024]{1,0:T(8,128)S(1)} %get-tuple-element.9.ends_ref) | copy-start | bytes 1572868
  27.4 4.0 %collective-permute-start.5 = (bf16[16,1024]{1,0:T(8,128)(2,1)S(1)}, bf16[16,1024]{1,0:T(8,128)(2,1)S(1)}, u32[]{:S(2)}, u32[]{:S(2)}) collective-permute-start(bf16[16,1024]{1,0:T(8,128)(2,1)S(1)} %convert_element_type.66), channel_id=1, source_target_pairs={{0,6},{2,0},{4,2},{6,4},{1,7},{3,1},{5,3},{7,5},{8,14},{10,8},{12,... | collective-permute-start | bytes 98312 | tf_op jit(solution)/shard_map/ppermute | solution.py:327
  30.4 4.3 %collective-permute-start.4 = (bf16[16,1024]{1,0:T(8,128)(2,1)S(1)}, bf16[16,1024]{1,0:T(8,128)(2,1)S(1)}, u32[]{:S(2)}, u32[]{:S(2)}) collective-permute-start(bf16[16,1024]{1,0:T(8,128)(2,1)S(1)} %convert_element_type.66), channel_id=1, source_target_pairs={{0,4},{2,6},{4,0},{6,2},{1,5},{3,7},{5,1},{7,3},{8,12},{10,14},{12... | collective-permute-start | bytes 98312 | tf_op jit(solution)/shard_map/ppermute | solution.py:327
  30.9 4.1 %collective-permute-start.3 = (bf16[16,1024]{1,0:T(8,128)(2,1)S(1)}, bf16[16,1024]{1,0:T(8,128)(2,1)S(1)}, u32[]{:S(2)}, u32[]{:S(2)}) collective-permute-start(bf16[16,1024]{1,0:T(8,128)(2,1)S(1)} %convert_element_type.66), channel_id=1, source_target_pairs={{0,2},{2,4},{4,6},{6,0},{1,3},{3,5},{5,7},{7,1},{8,10},{10,12},{12... | collective-permute-start | bytes 98312 | tf_op jit(solution)/shard_map/ppermute | solution.py:327
  35.1 4.0 %collective-permute-start.8 = (bf16[16,1024]{1,0:T(8,128)(2,1)S(1)}, bf16[16,1024]{1,0:T(8,128)(2,1)S(1)}, u32[]{:S(2)}, u32[]{:S(2)}) collective-permute-start(bf16[16,1024]{1,0:T(8,128)(2,1)S(1)} %get-tuple-element.14), channel_id=1, source_target_pairs={{0,24},{8,0},{16,8},{24,16},{1,25},{9,1},{17,9},{25,17},{2,26},{10... | collective-permute-start | bytes 98312 | tf_op jit(solution)/shard_map/ppermute | solution.py:327
  38.1 4.3 %collective-permute-start.7 = (bf16[16,1024]{1,0:T(8,128)(2,1)S(1)}, bf16[16,1024]{1,0:T(8,128)(2,1)S(1)}, u32[]{:S(2)}, u32[]{:S(2)}) collective-permute-start(bf16[16,1024]{1,0:T(8,128)(2,1)S(1)} %get-tuple-element.14), channel_id=1, source_target_pairs={{0,16},{8,24},{16,0},{24,8},{1,17},{9,25},{17,1},{25,9},{2,18},{10... | collective-permute-start | bytes 98312 | tf_op jit(solution)/shard_map/ppermute | solution.py:327
  38.4 4.3 %collective-permute-start.6 = (bf16[16,1024]{1,0:T(8,128)(2,1)S(1)}, bf16[16,1024]{1,0:T(8,128)(2,1)S(1)}, u32[]{:S(2)}, u32[]{:S(2)}) collective-permute-start(bf16[16,1024]{1,0:T(8,128)(2,1)S(1)} %get-tuple-element.14), channel_id=1, source_target_pairs={{0,8},{8,16},{16,24},{24,0},{1,9},{9,17},{17,25},{25,1},{2,10},{10... | collective-permute-start | bytes 98312 | tf_op jit(solution)/shard_map/ppermute | solution.py:327
  42.8 17.7 %collective-permute-start.11 = (bf16[16,1024]{1,0:T(8,128)(2,1)S(1)}, bf16[16,1024]{1,0:T(8,128)(2,1)S(1)}, u32[]{:S(2)}, u32[]{:S(2)}) collective-permute-start(bf16[16,1024]{1,0:T(8,128)(2,1)S(1)} %fusion.14), channel_id=1, source_target_pairs={{0,96},{32,0},{64,32},{96,64},{1,97},{33,1},{65,33},{97,65},{2,98}... | collective-permute-start | bytes 98312 | tf_op jit(solution)/shard_map/ppermute | solution.py:327
  46.6 13.9 %collective-permute-start.10 = (bf16[16,1024]{1,0:T(8,128)(2,1)S(1)}, bf16[16,1024]{1,0:T(8,128)(2,1)S(1)}, u32[]{:S(2)}, u32[]{:S(2)}) collective-permute-start(bf16[16,1024]{1,0:T(8,128)(2,1)S(1)} %fusion.14), channel_id=1, source_target_pairs={{0,64},{32,96},{64,0},{96,32},{1,65},{33,97},{65,1},{97,33},{2,66}... | collective-permute-start | bytes 98312 | tf_op jit(solution)/shard_map/ppermute | solution.py:327
  46.6 13.9 %collective-permute-start.9 = (bf16[16,1024]{1,0:T(8,128)(2,1)S(1)}, bf16[16,1024]{1,0:T(8,128)(2,1)S(1)}, u32[]{:S(2)}, u32[]{:S(2)}) collective-permute-start(bf16[16,1024]{1,0:T(8,128)(2,1)S(1)} %fusion.14), channel_id=1, source_target_pairs={{0,32},{32,64},{64,96},{96,0},{1,33},{33,65},{65,97},{97,1},{2,34}... | collective-permute-start | bytes 98312 | tf_op jit(solution)/shard_map/ppermute | solution.py:327
  47.4 1.6 %copy-start.2 = (bf16[528,2048]{1,0:T(8,128)(2,1)S(1)}, bf16[528,2048]{1,0:T(8,128)(2,1)}, u32[]{:S(2)}) copy-start(bf16[528,2048]{1,0:T(8,128)(2,1)} %get-tuple-element.12.lhs_ref) | copy-start | bytes 6488068
  55.2 5.5 %copy-start.5 = (f32[128,1024]{1,0:T(8,128)S(1)}, f32[128,1024]{1,0:T(8,128)}, u32[]{:S(2)}) copy-start(f32[128,1024]{1,0:T(8,128)} %copy-done.4) | copy-start | bytes 1572868
  65.0 7.2 %collective-permute-start.12 = (bf16[512,1024]{1,0:T(8,128)(2,1)S(1)}, bf16[512,1024]{1,0:T(8,128)(2,1)S(1)}, u32[]{:S(2)}, u32[]{:S(2)}) collective-permute-start(bf16[512,1024]{1,0:T(8,128)(2,1)S(1)} %hidden.1.own_ref), channel_id=1, source_target_pairs={{0,1},{1,0},{2,3},{3,2},{4,5},{5,4},{6,7},{7,6},{8,9},{9,8},{10,11... | collective-permute-start | bytes 3145736 | tf_op jit(solution)/shard_map/ppermute | solution.py:310
